TPU v7x, 32 devices: a whole 2x2x4 slice. The times are simulated.
32 devices in a mesh: row: 2 (over x), col: 16 (over z, y, core).
Axes of the slice: x: 2, y: 2, z: 4, core: 2. Of those that a mesh axis runs over, the one named last changes fastest.
Arguments:
- diagonal_tile: float32 [512, 512], P('row'), may hold values from -1 to 8, as said below
- panel: float32 [2048, 512], P(('row', 'col')), may hold values from -2.5 to 2.5
- trailing: bfloat16 [2048, 2048], P('col', 'row'), may hold values from -6 to 6
Outputs:
- factor_panel: float32 [2048, 512], P(('row', 'col'))
- updated: bfloat16 [2048, 2048], P('col', 'row')
Inputs may be any that keep to these rules, and one draw needn't show every extreme that they name: `diagonal_tile`: symmetric, and every eigenvalue is at least 1.
All inputs are finite; a program needn't handle non-finite values.
Results may differ from a plain program's by a relative error of at most 0.0085.
Values may be sent and summed in bfloat16 or wider, within the bound.
A program may use at most 64 MiB of HBM per device.

v0:
```python
import jax
import jax.numpy as jnp
from jax import lax
from jax.sharding import PartitionSpec as P


def per_device(diagonal_tile, panel, trailing):
    tile_whole = lax.all_gather(diagonal_tile, "row", axis=0, tiled=True)
    diag_factor = jnp.linalg.cholesky(tile_whole)

    def solve_rows(panel_rows):
        return jax.scipy.linalg.solve_triangular(diag_factor, panel_rows.T, lower=True).T

    factor_panel = solve_rows(panel)
    low_panel = factor_panel.astype(jnp.bfloat16)
    raw_rows = lax.all_gather(panel.astype(jnp.bfloat16), "row", axis=0, tiled=True).astype(
        panel.dtype
    )
    column_low = solve_rows(raw_rows).astype(jnp.bfloat16)
    block_low = lax.all_gather(low_panel, "col", axis=0, tiled=True)
    outer_term = lax.dot_general(
        column_low, block_low, (((1,), (1,)), ((), ())), preferred_element_type=jnp.float32
    )
    updated = (trailing.astype(jnp.float32) - outer_term).astype(jnp.bfloat16)
    return (factor_panel, updated)


def solution(mesh):
    return jax.shard_map(
        per_device,
        mesh=mesh,
        in_specs=(P("row", None), P(("row", "col"), None), P("col", "row")),
        out_specs=(P(("row", "col"), None), P("col", "row")),
        check_vma=False,
    )
```

profile of v0, /device:TPU:0, one launch (start us, length us, event | category | flops | bytes accessed | tf_op | source)
XLA Modules:
  0.0 216.5 jit_solution(180372973036767981)
XLA Ops:
  7.2 2.1 copy.5
  9.4 24.2 %all-gather.3.cloned.1.call-done = f32[512,512]{0,1:T(8,128)} async-done(((f32[256,512]{0,1:T(8,128)}), f32[512,512]{0,1:T(8,128)}) %all-gather.3.cloned.1.call-update) | async-done | bytes 1048592 | tf_op jit(solution)/shard_map/all_gather | solution.py:8
  33.6 1.6 copy.6
  35.2 0.2 fusion.1
  35.5 11.7 %cholesky.104 = f32[128,128]{1,0:T(8,128)S(1)} custom-call(f32[128,128]{1,0:T(8,128)S(1)} %cholesky.266), custom_call_target="Cholesky" | custom-call | tf_op jit(solution)/shard_map/jit(cholesky)/cholesky | solution.py:9
  47.2 9.8 %custom-call.34 = f32[1,128,128]{1,2,0:T(8,128)S(1)} custom-call(f32[1,128,128]{2,1,0:T(8,128)S(1)} %get-tuple-element.31), custom_call_target="InvertDiagBlocksLowerTriangular" | custom-call | tf_op jit(solution)/shard_map/jit(cholesky)/cholesky | solution.py:9
  57.2 0.3 constant_dynamic-update-slice_fusion.3
  57.5 0.3 convolution_subtract_fusion.1
  57.8 11.7 %cholesky.217 = f32[128,128]{1,0:T(8,128)S(1)} custom-call(f32[128,128]{1,0:T(8,128)S(1)} %cholesky.270), custom_call_target="Cholesky" | custom-call | tf_op jit(solution)/shard_map/jit(cholesky)/cholesky | solution.py:9
  69.6 10.0 %custom-call.35 = f32[1,128,128]{1,2,0:T(8,128)S(1)} custom-call(f32[1,128,128]{2,1,0:T(8,128)S(1)} %get-tuple-element.28), custom_call_target="InvertDiagBlocksLowerTriangular" | custom-call | tf_op jit(solution)/shard_map/jit(cholesky)/cholesky | solution.py:9
  79.5 0.3 convolution_dynamic-update-slice_fusion
  79.8 0.4 convolution_subtract_fusion.2
  80.2 11.7 %cholesky.238 = f32[128,128]{1,0:T(8,128)S(1)} custom-call(f32[128,128]{1,0:T(8,128)S(1)} %cholesky.275), custom_call_target="Cholesky" | custom-call | tf_op jit(solution)/shard_map/jit(cholesky)/cholesky | solution.py:9
  92.0 0.7 compare_reduce_fusion.1
  92.7 9.8 %custom-call.36 = f32[1,128,128]{1,2,0:T(8,128)S(1)} custom-call(f32[1,128,128]{2,1,0:T(8,128)S(1)} %get-tuple-element.25), custom_call_target="InvertDiagBlocksLowerTriangular" | custom-call | tf_op jit(solution)/shard_map/jit(cholesky)/cholesky | solution.py:9
  102.5 0.2 convolution_dynamic-update-slice_fusion.1
  102.7 0.4 convolution_subtract_fusion.6
  103.1 11.7 %cholesky.255 = f32[128,128]{1,0:T(8,128)S(1)} custom-call(f32[128,128]{1,0:T(8,128)S(1)} %convolution_subtract_fusion.6), custom_call_target="Cholesky" | custom-call | tf_op jit(solution)/shard_map/jit(cholesky)/cholesky | solution.py:9
  114.8 0.6 compare_reduce_fusion
  115.5 0.7 compare_reduce_fusion.2
  118.7 0.3 select_select_fusion
  119.0 8.5 %while.1 = (s32[]{:T(128)}, f32[512,512]{1,0:T(8,128)S(1)}, s32[4,2]{0,1:T(2,128)S(1)}, f32[4,128,128]{2,1,0:T(8,128)S(1)}, s32[]{:T(128)}) while((s32[]{:T(128)}, f32[512,512]{1,0:T(8,128)S(1)}, s32[4,2]{0,1:T(2,128)S(1)}, f32[4,128,128]{2,1,0:T(8,128)S(1)}, s32[]{:T(128)}) %tuple.35), condition=%wide.while_cond, body=%wide.while_body.sunk | while | flops 2 | bytes 131181 | solution.py:12
  119.1 0.6 fusion.72
  119.7 1.4 bitcast_dynamic-update-slice_fusion.2
  121.3 0.6 fusion.72
  121.9 1.4 bitcast_dynamic-update-slice_fusion.2
  123.4 0.6 fusion.72
  124.0 1.4 bitcast_dynamic-update-slice_fusion.2
  125.5 0.6 fusion.72
  126.1 1.4 bitcast_dynamic-update-slice_fusion.2
  127.5 39.3 %custom-call.37 = f32[4,128,128]{1,2,0:T(8,128)S(1)} custom-call(f32[4,128,128]{2,1,0:T(8,128)S(1)} %get-tuple-element.9), custom_call_target="InvertDiagBlocksLowerTriangular" | custom-call | tf_op jit(solution)/shard_map/jit(_solve_triangular)/triangular_solve | solution.py:12
  167.1 0.2 convolution_subtract_fusion.9
  167.3 0.2 fusion.43
  167.5 0.3 convolution_subtract_fusion.8
  167.8 0.2 fusion.45
  168.0 0.4 convolution_subtract_fusion.7
  168.4 0.2 fusion.46
  168.6 0.7 fusion.56
  169.3 4.9 %all_gather.10 = bf16[128,512]{1,0:T(8,128)(2,1)S(1)} all-gather(bf16[64,512]{1,0:T(8,128)(2,1)S(1)} %convert_element_type.16), channel_id=1, replica_groups=mesh['row'=2,'col'=16] {'row'}, dimensions={0}, use_global_device_ids=true | all-gather | bytes 196608 | tf_op jit(solution)/shard_map/all_gather | solution.py:16
  174.2 0.3 fusion.60
  174.5 0.3 convolution_subtract_fusion.4
  174.8 0.3 fusion.59
  175.1 0.4 convolution_subtract_fusion.3
  175.5 0.3 fusion.58
  175.8 0.5 convolution_subtract_fusion.5
  176.3 0.3 convolution_convert_fusion
  176.6 30.7 %all-gather.5.cloned.1.call-done = bf16[1024,512]{1,0:T(8,128)(2,1)} async-done(((bf16[64,512]{1,0:T(8,128)(2,1)}), bf16[1024,512]{1,0:T(8,128)(2,1)}) %all-gather.5.cloned.1.call-update) | async-done | bytes 1048592 | tf_op jit(solution)/shard_map/all_gather | solution.py:20
  207.3 2.4 %fusion = bf16[128,1024]{1,0:T(8,128)(2,1)} fusion(bf16[1024,512]{1,0:T(8,128)(2,1)} %all-gather.5.cloned.1.call-done, bf16[128,1024]{1,0:T(8,128)(2,1)S(1)} %copy-done.2, bf16[128,128]{1,0:T(8,128)(2,1)S(1)} %convolution_convert_fusion, bf16[128,128]{1,0:T(8,128)(2,1)S(1)} %get-tuple-element.34, bf16[128,128]{1,0:T(8,128)(2,1)S(1)} %get-tuple-element.36, ...), kind=kOutput, calls=%fused_computation.3 | convolution fusion | flops 135135232 | bytes 1703936 | tf_op jit(solution)/shard_map/dot_general | solution.py:21
  (28 shorter events, 0.9 us)
Async XLA Ops:
  7.2 26.4 %all-gather.3.cloned.1.call-start = ((), (), s32[]{:S(2)}) async-start(), calls=%async_computation | async-start | bytes 1572864 | tf_op jit(solution)/shard_map/all_gather | solution.py:8
  9.3 198.0 %all-gather.5.cloned.1.call-start = ((), (), s32[]{:S(2)}) async-start(), calls=%async_computation.1 | async-start | bytes 1114112 | tf_op jit(solution)/shard_map/all_gather | solution.py:20
  33.6 1.7 copy-start
  119.0 47.8 %copy-start.1 = (f32[64,512]{1,0:T(8,128)S(1)}, f32[64,512]{1,0:T(8,128)}, u32[]{:S(2)}) copy-start(f32[64,512]{1,0:T(8,128)} %param.4) | copy-start | bytes 393220
  175.8 31.5 %copy-start.2 = (bf16[128,1024]{1,0:T(8,128)(2,1)S(1)}, bf16[128,1024]{1,0:T(8,128)(2,1)}, u32[]{:S(2)}) copy-start(bf16[128,1024]{1,0:T(8,128)(2,1)} %param.5) | copy-start | bytes 786436
Sparse Core Ops, SparseCore 0:
  9.5 23.9 all-gather.2
  169.4 37.8 all-gather.4
where the time goes:
time: 217 us
  other arithmetic  119 us (55%)
  waiting for transfers between devices  54.9 us (25%)
  between operations  16.9 us (8%)
  local copies, waits for them, and re-layouts  12.3 us (6%)
  matrix products  8.2 us (4%)
  blocking collectives  4.93 us (2%)
    another operation x14, other arithmetic, per_device(): diag_factor = jnp.linalg.cholesky(tile_whole)  78.6 us
    another operation x3, other arithmetic, solve_rows(): jax.scipy.linalg.solve_triangular(diag_factor, panel_rows.T, lower=True)  39.7 us
    all_gather x1, waiting for transfers between devices, per_device(): block_low = lax.all_gather(low_panel, 'col', axis=0, tiled=True)  30.7 us
    all_gather x1, waiting for transfers between devices, per_device(): tile_whole = lax.all_gather(diagonal_tile, 'row', axis=0, tiled=True)  24.2 us
    another operation x12, local copies, waits for them, and re-layouts  8.39 us
    all_gather x1, blocking collectives, per_device(): lax.all_gather(panel.astype(jnp.bfloat16), 'row', axis=0, tiled=True)  4.93 us
  transfers between devices with their start and end apart: 2, of which 2 were waited for; matrix products, arithmetic and copies ran while one was open for 1% of the time, Pallas kernels for 0%

commit v1 on v0

--- a/solution.py
+++ b/solution.py
@@ -17,7 +17,8 @@
         panel.dtype
     )
     column_low = solve_rows(raw_rows).astype(jnp.bfloat16)
-    block_low = lax.all_gather(low_panel, "col", axis=0, tiled=True)
+    stack = jnp.stack([low_panel] * lax.axis_size("col"))
+    block_low = jnp.concatenate(lax.all_to_all(stack, "col", 0, 0), axis=0)
     outer_term = lax.dot_general(
         column_low, block_low, (((1,), (1,)), ((), ())), preferred_element_type=jnp.float32
     )

time: 217 us -> 208 us (0.959)
  waiting for transfers between devices: 54.9 us -> 39.7 us
  starting transfers between devices: 0.08 us -> 5.66 us
    all_gather x1 -> x0, waiting for transfers between devices: 30.7 us -> none  [per_device(): block_low = lax.all_gather(low_panel, 'col', axis=0, tiled=True)]
    all_to_all x0 -> x1, waiting for transfers between devices: none -> 15.4 us  [per_device(): block_low = jnp.concatenate(lax.all_to_all(stack, 'col', 0, 0), axis=0)]
    all_to_all x0 -> x1, starting transfers between devices: none -> 5.62 us  [per_device(): block_low = jnp.concatenate(lax.all_to_all(stack, 'col', 0, 0), axis=0)]
    another operation x12 -> x13, local copies, waits for them, and re-layouts: 8.39 us -> 9.48 us
where the time goes in v1:
time: 208 us; the launch traced here: 207 us
  other arithmetic  119 us (57%)
  waiting for transfers between devices  39.7 us (19%)
  between operations  16.9 us (8%)
  local copies, waits for them, and re-layouts  13.3 us (6%)
  matrix products  6.98 us (3%)
  starting transfers between devices  5.66 us (3%)
  blocking collectives  5.07 us (2%)
    another operation x14, other arithmetic, per_device(): diag_factor = jnp.linalg.cholesky(tile_whole)  78.8 us
    another operation x3, other arithmetic, solve_rows(): jax.scipy.linalg.solve_triangular(diag_factor, panel_rows.T, lower=True)  39.4 us
    all_gather x1, waiting for transfers between devices, per_device(): tile_whole = lax.all_gather(diagonal_tile, 'row', axis=0, tiled=True)  24.2 us
    all_to_all x1, waiting for transfers between devices, per_device(): block_low = jnp.concatenate(lax.all_to_all(stack, 'col', 0, 0), axis=0)  15.4 us
    another operation x12, local copies, waits for them, and re-layouts  8.39 us
    all_to_all x1, starting transfers between devices, per_device(): block_low = jnp.concatenate(lax.all_to_all(stack, 'col', 0, 0), axis=0)  5.62 us
    all_gather x1, blocking collectives, per_device(): lax.all_gather(panel.astype(jnp.bfloat16), 'row', axis=0, tiled=True)  5.07 us
  transfers between devices with their start and end apart: 2, of which 2 were waited for; matrix products, arithmetic and copies ran while one was open for 1% of the time, Pallas kernels for 0%

profile of v1, /device:TPU:0, one launch (start us, length us, event | category | flops | bytes accessed | tf_op | source)
XLA Modules:
  0.0 206.8 jit_solution(14678621344720530931)
XLA Ops:
  7.2 2.1 copy.5
  9.3 24.2 %all-gather.2.cloned.1.call-done = f32[512,512]{0,1:T(8,128)} async-done(((f32[256,512]{0,1:T(8,128)}), f32[512,512]{0,1:T(8,128)}) %all-gather.2.cloned.1.call-update) | async-done | bytes 1048592 | tf_op jit(solution)/shard_map/all_gather | solution.py:8
  33.6 1.6 copy.6
  35.2 0.2 fusion.1
  35.5 11.7 %cholesky.104 = f32[128,128]{1,0:T(8,128)S(1)} custom-call(f32[128,128]{1,0:T(8,128)S(1)} %cholesky.266), custom_call_target="Cholesky" | custom-call | tf_op jit(solution)/shard_map/jit(cholesky)/cholesky | solution.py:9
  47.2 9.8 %custom-call.34 = f32[1,128,128]{1,2,0:T(8,128)S(1)} custom-call(f32[1,128,128]{2,1,0:T(8,128)S(1)} %get-tuple-element.31), custom_call_target="InvertDiagBlocksLowerTriangular" | custom-call | tf_op jit(solution)/shard_map/jit(cholesky)/cholesky | solution.py:9
  57.2 0.3 constant_dynamic-update-slice_fusion.3
  57.5 0.3 convolution_subtract_fusion.1
  57.8 11.7 %cholesky.217 = f32[128,128]{1,0:T(8,128)S(1)} custom-call(f32[128,128]{1,0:T(8,128)S(1)} %cholesky.270), custom_call_target="Cholesky" | custom-call | tf_op jit(solution)/shard_map/jit(cholesky)/cholesky | solution.py:9
  69.6 9.9 %custom-call.35 = f32[1,128,128]{1,2,0:T(8,128)S(1)} custom-call(f32[1,128,128]{2,1,0:T(8,128)S(1)} %get-tuple-element.28), custom_call_target="InvertDiagBlocksLowerTriangular" | custom-call | tf_op jit(solution)/shard_map/jit(cholesky)/cholesky | solution.py:9
  79.5 0.3 convolution_dynamic-update-slice_fusion
  79.8 0.4 convolution_subtract_fusion.2
  80.2 11.7 %cholesky.238 = f32[128,128]{1,0:T(8,128)S(1)} custom-call(f32[128,128]{1,0:T(8,128)S(1)} %cholesky.275), custom_call_target="Cholesky" | custom-call | tf_op jit(solution)/shard_map/jit(cholesky)/cholesky | solution.py:9
  91.9 0.7 compare_reduce_fusion.1
  92.7 9.8 %custom-call.36 = f32[1,128,128]{1,2,0:T(8,128)S(1)} custom-call(f32[1,128,128]{2,1,0:T(8,128)S(1)} %get-tuple-element.25), custom_call_target="InvertDiagBlocksLowerTriangular" | custom-call | tf_op jit(solution)/shard_map/jit(cholesky)/cholesky | solution.py:9
  102.5 0.2 convolution_dynamic-update-slice_fusion.1
  102.7 0.4 convolution_subtract_fusion.6
  103.1 11.7 %cholesky.255 = f32[128,128]{1,0:T(8,128)S(1)} custom-call(f32[128,128]{1,0:T(8,128)S(1)} %convolution_subtract_fusion.6), custom_call_target="Cholesky" | custom-call | tf_op jit(solution)/shard_map/jit(cholesky)/cholesky | solution.py:9
  114.8 0.8 compare_reduce_fusion
  115.7 0.7 compare_reduce_fusion.2
  119.0 8.5 %while.1 = (s32[]{:T(128)}, f32[512,512]{1,0:T(8,128)S(1)}, s32[4,2]{0,1:T(2,128)S(1)}, f32[4,128,128]{2,1,0:T(8,128)S(1)}, s32[]{:T(128)}) while((s32[]{:T(128)}, f32[512,512]{1,0:T(8,128)S(1)}, s32[4,2]{0,1:T(2,128)S(1)}, f32[4,128,128]{2,1,0:T(8,128)S(1)}, s32[]{:T(128)}) %tuple.35), condition=%wide.while_cond, body=%wide.while_body.sunk | while | flops 2 | bytes 131181 | solution.py:12
  119.1 0.6 fusion.72
  119.7 1.4 bitcast_dynamic-update-slice_fusion.2
  121.2 0.6 fusion.72
  121.8 1.4 bitcast_dynamic-update-slice_fusion.2
  123.4 0.6 fusion.72
  123.9 1.4 bitcast_dynamic-update-slice_fusion.2
  125.5 0.6 fusion.72
  126.1 1.4 bitcast_dynamic-update-slice_fusion.2
  127.5 39.3 %custom-call.37 = f32[4,128,128]{1,2,0:T(8,128)S(1)} custom-call(f32[4,128,128]{2,1,0:T(8,128)S(1)} %get-tuple-element.9), custom_call_target="InvertDiagBlocksLowerTriangular" | custom-call | tf_op jit(solution)/shard_map/jit(_solve_triangular)/triangular_solve | solution.py:12
  166.8 0.2 fusion.41
  167.0 0.2 convolution_subtract_fusion.9
  167.5 0.3 convolution_subtract_fusion.8
  167.7 0.2 fusion.45
  167.9 0.4 convolution_subtract_fusion.7
  168.5 0.7 fusion.56
  169.2 1.1 stack.2
  170.3 5.6 %all-to-all-start = ((bf16[16,64,512]{2,1,0:T(8,128)(2,1)}), bf16[16,64,512]{2,1,0:T(8,128)(2,1)S(1)}, u32[]{:S(2)}, u32[]{:S(2)}) async-start(bf16[16,64,512]{2,1,0:T(8,128)(2,1)} %stack.2), calls=%async_computation | async-start | bytes 2097152 | tf_op jit(solution)/shard_map/all_to_all | solution.py:21
  175.9 5.1 %all_gather.7 = bf16[128,512]{1,0:T(8,128)(2,1)S(1)} all-gather(bf16[64,512]{1,0:T(8,128)(2,1)S(1)} %convert_element_type.16), channel_id=1, replica_groups=mesh['row'=2,'col'=16] {'row'}, dimensions={0}, use_global_device_ids=true | all-gather | bytes 196608 | tf_op jit(solution)/shard_map/all_gather | solution.py:16
  181.0 0.2 fusion.60
  181.3 0.3 convolution_subtract_fusion.4
  181.6 0.3 fusion.59
  181.9 0.4 convolution_subtract_fusion.3
  182.3 0.3 fusion.58
  182.6 0.5 convolution_subtract_fusion.5
  183.1 0.3 convolution_convert_fusion
  183.4 15.4 %all-to-all-done = bf16[16,64,512]{2,1,0:T(8,128)(2,1)S(1)} async-done(((bf16[16,64,512]{2,1,0:T(8,128)(2,1)}), bf16[16,64,512]{2,1,0:T(8,128)(2,1)S(1)}, u32[]{:S(2)}, u32[]{:S(2)}) %all-to-all-start) | async-done | bytes 1048608 | tf_op jit(solution)/shard_map/all_to_all | solution.py:21
  198.8 1.2 fusion
  (28 shorter events, 1.2 us)
Async XLA Ops:
  7.2 26.4 %all-gather.2.cloned.1.call-start = ((), (), s32[]{:S(2)}) async-start(), calls=%async_computation.1 | async-start | bytes 1572864 | tf_op jit(solution)/shard_map/all_gather | solution.py:8
  33.6 1.7 copy-start
  119.0 47.8 %copy-start.1 = (f32[64,512]{1,0:T(8,128)S(1)}, f32[64,512]{1,0:T(8,128)}, u32[]{:S(2)}) copy-start(f32[64,512]{1,0:T(8,128)} %param.4) | copy-start | bytes 393220
  170.3 28.5 %all-to-all-start = ((bf16[16,64,512]{2,1,0:T(8,128)(2,1)}), bf16[16,64,512]{2,1,0:T(8,128)(2,1)S(1)}, u32[]{:S(2)}, u32[]{:S(2)}) async-start(bf16[16,64,512]{2,1,0:T(8,128)(2,1)} %stack.2), calls=%async_computation | async-start | bytes 2097152 | tf_op jit(solution)/shard_map/all_to_all | solution.py:21
  182.6 16.2 %copy-start.2 = (bf16[128,1024]{1,0:T(8,128)(2,1)S(1)}, bf16[128,1024]{1,0:T(8,128)(2,1)}, u32[]{:S(2)}) copy-start(bf16[128,1024]{1,0:T(8,128)(2,1)} %param.5) | copy-start | bytes 786436
Sparse Core Ops, SparseCore 0:
  9.5 23.9 all-gather.1
